TPU v7x, 32 devices: a whole 2x2x4 slice. The times are simulated.
32 devices in a mesh: sub: 8 (over z, y), col: 4 (over x, core).
Axes of the slice: x: 2, y: 2, z: 4, core: 2. Of those that a mesh axis runs over, the one named last changes fastest.
Arguments:
- rhs: bfloat16 [32, 1024, 128], P(('sub', 'col')), may hold values from -64 to 64
- schur: bfloat16 [32, 1024, 1024], P(('sub', 'col')), may hold values from -1 to 3
- local_inverse: bfloat16 [32, 1024, 1024], P(('sub', 'col')), may hold values from -1 to 2
- basis: bfloat16 [32, 8, 1024], P(('sub', 'col')), may hold values from -0.75 to 0.75
- coarse_inverse: bfloat16 [256, 256], P('sub', 'col'), may hold values from -1 to 2
- primal_index: int32 [32, 8], P(('sub', 'col')), may hold values from 0 to 255, as said below
- neighbour_dof: int32 [32, 1024], P(('sub', 'col')), may hold values from 0 to 1023, as said below
Outputs:
- solution: bfloat16 [32, 1024, 128], P(('sub', 'col'))
Inputs may be any that keep to these rules, and one draw needn't show every extreme that they name: `neighbour_dof`: each subdomain's unknowns in one shared block name places in the neighbour's facing block (for [0, 256) the neighbour's [256, 512), and so on), and the neighbour's entry names the place back. `primal_index`: every coarse unknown is named exactly once over all subdomains.
All inputs are finite; a program needn't handle non-finite values.
Results may differ from a plain program's by a relative error of at most 0.004.
The roundings to bfloat16 on the way count: a program that leaves them out, or rounds other values in their place, can miss the bound.
Values may be sent and summed in bfloat16 or wider, within the bound.
A program may use at most 64 MiB of HBM per device.

v0:
```python
import jax
import jax.numpy as jnp
from jax import lax
from jax.sharding import PartitionSpec as P


def from_behind(value, axis, steps):
    count = lax.axis_size(axis)
    pairs = [(source, (source + steps) % count) for source in range(count)]
    return lax.ppermute(value, axis, pairs)


def on_device(rhs, schur, local_inverse, basis, coarse_inverse, primal_index, neighbour_dof):
    link_table = neighbour_dof[0]
    face_size = link_table.shape[0] // 4
    cases = rhs.shape[2]
    offsets = (face_size, 0, 3 * face_size, 2 * face_size)
    places = []
    for number in range(4):
        places.append(link_table[number * face_size : (number + 1) * face_size] - offsets[number])
    schur_own = schur[0]
    inverse_own = local_inverse[0]
    basis_own = basis[0]
    index_own = primal_index[0]
    column_width = coarse_inverse.shape[1]
    column_base = lax.axis_index("col") * column_width

    def combine(field, incoming):
        collected = [
            jnp.take(incoming[number].astype(jnp.float32), places[number], axis=0)
            for number in range(4)
        ]
        return field + jnp.concatenate(collected, axis=0)

    def assemble(field):
        from_below = from_behind(field[face_size : 2 * face_size], "sub", 1)
        from_above = from_behind(field[:face_size], "sub", -1)
        from_left = from_behind(field[3 * face_size :].astype(jnp.bfloat16), "col", 1).astype(
            jnp.float32
        )
        from_right = from_behind(field[2 * face_size : 3 * face_size], "col", -1)
        return combine(field, (from_below, from_above, from_left, from_right))

    def inner(left_field, right_field):
        return lax.psum(0.5 * jnp.sum(left_field * right_field, axis=0), ("sub", "col"))

    residual = assemble(rhs[0].astype(jnp.float32))
    weighted = (residual * 0.5).astype(jnp.bfloat16)
    local_part = jnp.dot(inverse_own, weighted, preferred_element_type=jnp.float32)
    coarse_load = jnp.dot(basis_own, weighted, preferred_element_type=jnp.float32).astype(
        jnp.bfloat16
    )
    start_block = jnp.zeros((column_width, cases), jnp.bfloat16)
    values = lax.all_gather(coarse_load, ("sub", "col"), axis=0, tiled=True)
    indices = lax.all_gather(index_own, ("sub", "col"), axis=0, tiled=True)
    spots = indices - column_base
    spots = jnp.where((spots >= 0) & (spots < column_width), spots, column_width)
    column_part = start_block.at[spots].set(values, mode="drop")
    partial_rows = jnp.dot(coarse_inverse, column_part, preferred_element_type=jnp.float32)
    start_taken = jnp.zeros((index_own.shape[0], cases), jnp.bfloat16)
    block_rows = lax.psum(partial_rows, "col").astype(jnp.bfloat16)
    piece = lax.all_gather(block_rows, "sub", axis=0, tiled=True)
    spots = index_own
    count = piece.shape[0]
    valid = (spots >= 0) & (spots < count)
    rows = jnp.take(piece, jnp.clip(spots, 0, count - 1), axis=0)
    taken = jnp.where(valid[:, None], rows, start_taken)
    correction = lax.dot_general(
        basis_own, taken, (((0,), (0,)), ((), ())), preferred_element_type=jnp.float32
    )
    first = assemble((local_part + correction) * 0.5)
    rz_first = inner(residual, first)
    image = assemble(
        jnp.dot(schur_own, first.astype(jnp.bfloat16), preferred_element_type=jnp.float32)
    )
    alpha = rz_first / inner(first, image)
    return (alpha * first).astype(jnp.bfloat16)[None]


def solution(mesh):
    return jax.shard_map(
        on_device,
        mesh=mesh,
        in_specs=(
            P(("sub", "col"), None, None),
            P(("sub", "col"), None, None),
            P(("sub", "col"), None, None),
            P(("sub", "col"), None, None),
            P("sub", "col"),
            P(("sub", "col"), None),
            P(("sub", "col"), None),
        ),
        out_specs=P(("sub", "col"), None, None),
        check_vma=False,
    )
```

profile of v0, /device:TPU:0, one launch (start us, length us, event | category | flops | bytes accessed | tf_op | source)
XLA Modules:
  0.0 225.9 jit_solution(8289083633915082191)
XLA Ops:
  0.0 1.2 copy.8
  1.3 3.1 %collective-permute-start = (f32[256,128]{0,1:T(8,128)S(1)}, f32[256,128]{0,1:T(8,128)S(1)}, u32[]{:S(2)}, u32[]{:S(2)}) collective-permute-start(f32[256,128]{0,1:T(8,128)S(1)} %get-tuple-element.16), channel_id=1, source_target_pairs={{0,4},{4,8},{8,12},{12,16},{16,20},{20,24},{24,28},{28,0},{1,5},{5... | collective-permute-start | bytes 393224 | tf_op jit(solution)/shard_map/ppermute | solution.py:10
  4.4 3.1 %collective-permute-start.1 = (f32[256,128]{0,1:T(8,128)S(1)}, f32[256,128]{0,1:T(8,128)S(1)}, u32[]{:S(2)}, u32[]{:S(2)}) collective-permute-start(f32[256,128]{0,1:T(8,128)S(1)} %get-tuple-element.17), channel_id=1, source_target_pairs={{0,28},{4,0},{8,4},{12,8},{16,12},{20,16},{24,20},{28,24},{1,29},{... | collective-permute-start | bytes 393224 | tf_op jit(solution)/shard_map/ppermute | solution.py:10
  7.5 0.7 collective-permute-start.3
  8.1 0.8 slice_bitcast_fusion.3
  9.0 0.5 compare_and_fusion.3
  9.6 0.6 compare_and_fusion.2
  10.2 0.6 compare_and_fusion
  10.7 0.5 compare_and_fusion.1
  11.2 0.6 and_bitcast_fusion
  11.8 0.6 compare_and_fusion.4
  12.6 37.7 %all-reduce = s32[256]{0:T(256)S(1)} all-reduce(s32[256]{0:T(256)S(1)} %bitcast_dynamic-update-slice_fusion), channel_id=2, replica_groups=mesh['sub'=8,'col'=4] {'sub','col'}, use_global_device_ids=true, to_apply=%add | all-reduce | flops 256 | bytes 2048
  50.3 0.6 compare_select_fusion.4
  50.9 0.6 pad_clamp_fusion
  51.5 0.7 gather_fusion.3
  52.3 0.6 fusion.39
  52.9 1.2 broadcast_select_fusion.9
  54.3 0.7 gather_fusion.1
  55.2 0.7 gather_fusion.2
  56.2 0.7 gather_fusion.4
  57.2 0.2 fusion.9
  57.4 41.2 %all_gather.10 = bf16[256,128]{1,0:T(8,128)(2,1)S(1)} all-gather(bf16[8,128]{1,0:T(8,128)(2,1)S(1)} %fusion.9), channel_id=1, replica_groups=mesh['sub'=8,'col'=4] {'sub','col'}, dimensions={0}, use_global_device_ids=true | all-gather | bytes 67584 | tf_op jit(solution)/shard_map/all_gather | solution.py:54
  98.6 1.3 scatter_custom_fusion
  100.0 10.3 %psum.21 = bf16[32,128]{1,0:T(8,128)(2,1)S(1)} all-reduce(f32[32,128]{1,0:T(8,128)S(1)} %convolution_bitcast_fusion), channel_id=1, replica_groups=mesh['sub'=8,'col'=4] {'col'}, use_global_device_ids=true, to_apply=%region_1.3 | all-reduce | flops 4096 | bytes 24576 | tf_op jit(solution)/shard_map/psum | solution.py:61
  110.4 30.5 %all_gather.11 = bf16[256,128]{1,0:T(8,128)(2,1)S(1)} all-gather(bf16[32,128]{1,0:T(8,128)(2,1)S(1)} %psum.21), channel_id=1, replica_groups=mesh['sub'=8,'col'=4] {'sub'}, dimensions={0}, use_global_device_ids=true | all-gather | bytes 73728 | tf_op jit(solution)/shard_map/all_gather | solution.py:62
  140.9 1.6 fusion.2
  142.5 0.7 gather_fusion
  143.2 1.4 fusion.8
  144.6 0.8 fusion.34
  145.4 0.7 broadcast_select_fusion.10
  146.1 0.7 broadcast_select_fusion.11
  146.7 4.7 %collective-permute-start.5 = (f32[256,128]{0,1:T(8,128)}, f32[256,128]{0,1:T(8,128)S(1)}, u32[]{:S(2)}, u32[]{:S(2)}) collective-permute-start(f32[256,128]{0,1:T(8,128)} %get-tuple-element.15), channel_id=1, source_target_pairs={{0,28},{4,0},{8,4},{12,8},{16,12},{20,16},{24,20},{28,24},{1,29},{... | collective-permute-start | bytes 393224 | tf_op jit(solution)/shard_map/ppermute | solution.py:10
  151.4 0.5 collective-permute-start.6
  151.9 1.3 broadcast_select_fusion.8
  153.3 2.2 collective-permute-done.6
  155.5 0.7 gather_fusion.7
  156.5 0.7 gather_fusion.5
  157.4 0.7 gather_fusion.6
  158.3 1.0 copy.22
  159.3 0.7 gather_fusion.8
  160.1 0.8 broadcast_select_fusion.6
  161.0 0.7 broadcast_select_fusion.4
  161.8 0.8 fusion.4
  162.7 0.8 fusion.33
  163.4 2.0 collective-permute-start.9
  165.5 1.4 collective-permute-start.11
  166.9 0.9 copy.28
  167.8 1.3 gather_fusion.11
  169.2 1.0 copy.29
  170.2 1.2 broadcast_select_fusion.1
  171.4 1.0 copy.26
  172.4 1.4 gather_fusion.10
  173.8 1.0 copy.27
  174.8 1.3 broadcast_select_fusion.2
  176.1 1.0 copy.24
  177.1 1.3 gather_fusion.9
  178.5 1.0 copy.25
  179.5 0.7 broadcast_select_fusion.3
  180.1 1.0 copy.30
  181.1 1.3 gather_fusion.12
  182.5 1.0 copy.31
  183.5 1.5 fusion.15
  185.0 39.9 %all-reduce.1 = (f32[128]{0:T(128)S(1)}, f32[128]{0:T(128)S(1)}) all-reduce(f32[128]{0:T(128)S(1)} %broadcast_multiply_fusion.1, f32[128]{0:T(128)S(1)} %broadcast_multiply_fusion), channel_id=1, replica_groups=mesh['sub'=8,'col'=4] {'sub','col'}, use_global_device_ids=true, to_apply=%region_3.5 | all-reduce | flops 256 | bytes 2048 | tf_op jit(solution)/shard_map/psum | solution.py:45
  225.1 0.8 copy.32
  (84 shorter events, 2.2 us)
Async XLA Ops:
  0.0 140.9 %copy-start = (bf16[1,1024,1024]{2,1,0:T(8,128)(2,1)S(1)}, bf16[1,1024,1024]{2,1,0:T(8,128)(2,1)}, u32[]{:S(2)}) copy-start(bf16[1,1024,1024]{2,1,0:T(8,128)(2,1)} %param.11) | copy-start | bytes 6291460
  0.0 9.0 %copy-start.9 = (s32[1,1024]{1,0:T(1,128)S(1)}, s32[1,1024]{1,0:T(1,128)}, u32[]{:S(2)}) copy-start(s32[1,1024]{1,0:T(1,128)} %param.15) | copy-start | bytes 12292
  0.0 11.2 %copy-start.12 = (s32[1,8]{1,0:T(1,128)S(1)}, s32[1,8]{1,0:T(1,128)}, u32[]{:S(2)}) copy-start(s32[1,8]{1,0:T(1,128)} %param.14) | copy-start | bytes 100
  1.3 52.8 %collective-permute-start = (f32[256,128]{0,1:T(8,128)S(1)}, f32[256,128]{0,1:T(8,128)S(1)}, u32[]{:S(2)}, u32[]{:S(2)}) collective-permute-start(f32[256,128]{0,1:T(8,128)S(1)} %get-tuple-element.16), channel_id=1, source_target_pairs={{0,4},{4,8},{8,12},{12,16},{16,20},{20,24},{24,28},{28,0},{1,5},{5... | collective-permute-start | bytes 393224 | tf_op jit(solution)/shard_map/ppermute | solution.py:10
  4.4 50.7 %collective-permute-start.1 = (f32[256,128]{0,1:T(8,128)S(1)}, f32[256,128]{0,1:T(8,128)S(1)}, u32[]{:S(2)}, u32[]{:S(2)}) collective-permute-start(f32[256,128]{0,1:T(8,128)S(1)} %get-tuple-element.17), channel_id=1, source_target_pairs={{0,28},{4,0},{8,4},{12,8},{16,12},{20,16},{24,20},{28,24},{1,29},{... | collective-permute-start | bytes 393224 | tf_op jit(solution)/shard_map/ppermute | solution.py:10
  7.5 48.6 %collective-permute-start.3 = (f32[256,128]{0,1:T(8,128)S(1)}, f32[256,128]{0,1:T(8,128)S(1)}, u32[]{:S(2)}, u32[]{:S(2)}) collective-permute-start(f32[256,128]{0,1:T(8,128)S(1)} %get-tuple-element.18), channel_id=1, source_target_pairs={{0,3},{1,0},{2,1},{3,2},{4,7},{5,4},{6,5},{7,6},{8,11},{9,8},{10,9... | collective-permute-start | bytes 393224 | tf_op jit(solution)/shard_map/ppermute | solution.py:10
  9.0 42.5 %collective-permute-start.2 = (bf16[256,128]{1,0:T(8,128)(2,1)S(1)}, bf16[256,128]{1,0:T(8,128)(2,1)S(1)}, u32[]{:S(2)}, u32[]{:S(2)}) collective-permute-start(bf16[256,128]{1,0:T(8,128)(2,1)S(1)} %slice_bitcast_fusion.3), channel_id=1, source_target_pairs={{0,1},{1,2},{2,3},{3,0},{4,5},{5,6},{6,7},{7,4},{8,9},{9,10},{10,1... | collective-permute-start | bytes 196616 | tf_op jit(solution)/shard_map/ppermute | solution.py:10
  55.0 2.0 copy-start.6
  55.0 2.1 copy-start.8
  55.0 2.1 copy-start.4
  56.0 1.3 copy-start.2
  56.0 43.9 %copy-start.3 = (bf16[32,64]{1,0:T(8,128)(2,1)S(1)}, bf16[32,64]{1,0:T(8,128)(2,1)}, u32[]{:S(2)}) copy-start(bf16[32,64]{1,0:T(8,128)(2,1)} %param.13) | copy-start | bytes 12292
  57.1 86.1 %copy-start.10 = (pred[8]{0:T(512)(128)(4,1)S(1)}, pred[8]{0:T(512)(128)(4,1)}, u32[]{:S(2)}) copy-start(pred[8]{0:T(512)(128)(4,1)} %and_bitcast_fusion) | copy-start | bytes 28
  57.1 86.1 %copy-start.11 = (pred[8]{0:T(512)(128)(4,1)S(1)}, pred[8]{0:T(512)(128)(4,1)}, u32[]{:S(2)}) copy-start(pred[8]{0:T(512)(128)(4,1)} %compare_and_fusion.4) | copy-start | bytes 28
  146.7 9.7 %collective-permute-start.4 = (f32[256,128]{0,1:T(8,128)}, f32[256,128]{0,1:T(8,128)S(1)}, u32[]{:S(2)}, u32[]{:S(2)}) collective-permute-start(f32[256,128]{0,1:T(8,128)} %get-tuple-element.13), channel_id=1, source_target_pairs={{0,4},{4,8},{8,12},{12,16},{16,20},{20,24},{24,28},{28,0},{1,5},{5... | collective-permute-start | bytes 393224 | tf_op jit(solution)/shard_map/ppermute | solution.py:10
  146.7 10.6 %collective-permute-start.5 = (f32[256,128]{0,1:T(8,128)}, f32[256,128]{0,1:T(8,128)S(1)}, u32[]{:S(2)}, u32[]{:S(2)}) collective-permute-start(f32[256,128]{0,1:T(8,128)} %get-tuple-element.15), channel_id=1, source_target_pairs={{0,28},{4,0},{8,4},{12,8},{16,12},{20,16},{24,20},{28,24},{1,29},{... | collective-permute-start | bytes 393224 | tf_op jit(solution)/shard_map/ppermute | solution.py:10
  151.4 6.8 %collective-permute-start.7 = (f32[256,128]{0,1:T(8,128)}, f32[256,128]{0,1:T(8,128)}, u32[]{:S(2)}, u32[]{:S(2)}) collective-permute-start(f32[256,128]{0,1:T(8,128)} %get-tuple-element.14), channel_id=1, source_target_pairs={{0,3},{1,0},{2,1},{3,2},{4,7},{5,4},{6,5},{7,6},{8,11},{9,8},{10,9... | collective-permute-start | bytes 393224 | tf_op jit(solution)/shard_map/ppermute | solution.py:10
  151.4 4.0 %collective-permute-start.6 = (bf16[256,128]{0,1:T(8,128)(2,1)S(1)}, bf16[256,128]{0,1:T(8,128)(2,1)S(1)}, u32[]{:S(2)}, u32[]{:S(2)}) collective-permute-start(bf16[256,128]{0,1:T(8,128)(2,1)S(1)} %slice.134), channel_id=1, source_target_pairs={{0,1},{1,2},{2,3},{3,0},{4,5},{5,6},{6,7},{7,4},{8,9},{9,10},{10,1... | collective-permute-start | bytes 196616 | tf_op jit(solution)/shard_map/ppermute | solution.py:10
  160.1 1.6 copy-start.1
  162.6 4.3 %collective-permute-start.10 = (bf16[256,128]{0,1:T(8,128)(2,1)S(1)}, bf16[256,128]{0,1:T(8,128)(2,1)}, u32[]{:S(2)}, u32[]{:S(2)}) collective-permute-start(bf16[256,128]{0,1:T(8,128)(2,1)S(1)} %slice.133), channel_id=1, source_target_pairs={{0,1},{1,2},{2,3},{3,0},{4,5},{5,6},{6,7},{7,4},{8,9},{9,10},{10,1... | collective-permute-start | bytes 196616 | tf_op jit(solution)/shard_map/ppermute | solution.py:10
  163.4 8.0 %collective-permute-start.9 = (f32[256,128]{0,1:T(8,128)}, f32[256,128]{0,1:T(8,128)}, u32[]{:S(2)}, u32[]{:S(2)}) collective-permute-start(f32[256,128]{0,1:T(8,128)} %get-tuple-element.12), channel_id=1, source_target_pairs={{0,28},{4,0},{8,4},{12,8},{16,12},{20,16},{24,20},{28,24},{1,29},{... | collective-permute-start | bytes 393224 | tf_op jit(solution)/shard_map/ppermute | solution.py:10
  165.4 10.7 %collective-permute-start.8 = (f32[256,128]{0,1:T(8,128)}, f32[256,128]{0,1:T(8,128)}, u32[]{:S(2)}, u32[]{:S(2)}) collective-permute-start(f32[256,128]{0,1:T(8,128)} %get-tuple-element.10), channel_id=1, source_target_pairs={{0,4},{4,8},{8,12},{12,16},{16,20},{20,24},{24,28},{28,0},{1,5},{5... | collective-permute-start | bytes 393224 | tf_op jit(solution)/shard_map/ppermute | solution.py:10
  165.5 14.7 %collective-permute-start.11 = (f32[256,128]{0,1:T(8,128)}, f32[256,128]{0,1:T(8,128)}, u32[]{:S(2)}, u32[]{:S(2)}) collective-permute-start(f32[256,128]{0,1:T(8,128)} %get-tuple-element.11), channel_id=1, source_target_pairs={{0,3},{1,0},{2,1},{3,2},{4,7},{5,4},{6,5},{7,6},{8,11},{9,8},{10,9... | collective-permute-start | bytes 393224 | tf_op jit(solution)/shard_map/ppermute | solution.py:10
  169.2 10.3 %copy-start.7 = (pred[256]{0:T(512)(128)(4,1)S(1)}, pred[256]{0:T(512)(128)(4,1)}, u32[]{:S(2)}) copy-start(pred[256]{0:T(512)(128)(4,1)} %compare_and_fusion.3) | copy-start | bytes 772
  173.8 9.7 %copy-start.5 = (pred[256]{0:T(512)(128)(4,1)S(1)}, pred[256]{0:T(512)(128)(4,1)}, u32[]{:S(2)}) copy-start(pred[256]{0:T(512)(128)(4,1)} %compare_and_fusion) | copy-start | bytes 772
where the time goes:
time: 227 us; the launch traced here: 226 us
  blocking collectives  160 us (70%)
  local copies, waits for them, and re-layouts  28.1 us (12%)
  other arithmetic  15.7 us (7%)
  starting transfers between devices  15.5 us (7%)
  matrix products  4.13 us (2%)
    all_gather x1, blocking collectives, on_device(): values = lax.all_gather(coarse_load, ('sub', 'col'), axis=0, tiled=True)  41.2 us
    psum x1, blocking collectives, inner(): lax.psum(0.5 * jnp.sum(left_field * right_field, axis=0), ('sub', 'col'))  39.9 us
    unnamed x1, blocking collectives  37.7 us
    all_gather x1, blocking collectives, on_device(): piece = lax.all_gather(block_rows, 'sub', axis=0, tiled=True)  30.5 us
    gather x24, local copies, waits for them, and re-layouts, combine(): jnp.take(incoming[number].astype(jnp.float32), places[number], axis=0)  16 us
    ppermute x12, starting transfers between devices, from_behind(): return lax.ppermute(value, axis, pairs)  15.5 us
    psum x1, blocking collectives, on_device(): block_rows = lax.psum(partial_rows, 'col').astype(jnp.bfloat16)  10.3 us
    select_n x14, other arithmetic, combine(): jnp.take(incoming[number].astype(jnp.float32), places[number], axis=0)  8.71 us
  transfers between devices with their start and end apart: 12, of which 1 were waited for; matrix products, arithmetic and copies ran while one was open for 12% of the time, Pallas kernels for 0%

commit v1 on v0

--- a/solution.py
+++ b/solution.py
@@ -2,6 +2,12 @@
 import jax.numpy as jnp
 from jax import lax
 from jax.sharding import PartitionSpec as P
+
+
+def add_all(block, axis):
+    pieces = lax.all_gather(block, axis, axis=0, tiled=False)
+    total = pieces.sum(axis=0)
+    return total
 
 
 def from_behind(value, axis, steps):
@@ -42,7 +48,7 @@
         return combine(field, (from_below, from_above, from_left, from_right))
 
     def inner(left_field, right_field):
-        return lax.psum(0.5 * jnp.sum(left_field * right_field, axis=0), ("sub", "col"))
+        return add_all(0.5 * jnp.sum(left_field * right_field, axis=0), ("sub", "col"))
 
     residual = assemble(rhs[0].astype(jnp.float32))
     weighted = (residual * 0.5).astype(jnp.bfloat16)

time: 227 us -> 265 us (1.17)
  blocking collectives: 160 us -> 198 us
    all_gather x0 -> x2, blocking collectives: none -> 78.5 us  [add_all(): pieces = lax.all_gather(block, axis, axis=0, tiled=False)]
    psum x1 -> x0, blocking collectives: 39.9 us -> none  [inner(): lax.psum(0.5 * jnp.sum(left_field * right_field, axis=0), ('sub', 'col'))]
  transfers between devices with their start and end apart: 12 -> 12, of which waited for: 1 -> 1; matrix products, arithmetic and copies ran while one was open for 12% -> 11% of each run, Pallas kernels for 0% -> 0%
where the time goes in v1:
time: 265 us; the launch traced here: 264 us
  blocking collectives  198 us (75%)
  local copies, waits for them, and re-layouts  28.1 us (11%)
  other arithmetic  15.5 us (6%)
  starting transfers between devices  15.5 us (6%)
  matrix products  4.13 us (2%)
    all_gather x2, blocking collectives, add_all(): pieces = lax.all_gather(block, axis, axis=0, tiled=False)  78.5 us
    all_gather x1, blocking collectives, on_device(): values = lax.all_gather(coarse_load, ('sub', 'col'), axis=0, tiled=True)  41.2 us
    unnamed x1, blocking collectives  37.7 us
    all_gather x1, blocking collectives, on_device(): piece = lax.all_gather(block_rows, 'sub', axis=0, tiled=True)  30.5 us
    gather x24, local copies, waits for them, and re-layouts, combine(): jnp.take(incoming[number].astype(jnp.float32), places[number], axis=0)  16 us
    ppermute x12, starting transfers between devices, from_behind(): return lax.ppermute(value, axis, pairs)  15.5 us
    psum x1, blocking collectives, on_device(): block_rows = lax.psum(partial_rows, 'col').astype(jnp.bfloat16)  10.3 us
    select_n x14, other arithmetic, combine(): jnp.take(incoming[number].astype(jnp.float32), places[number], axis=0)  8.59 us
  transfers between devices with their start and end apart: 12, of which 1 were waited for; matrix products, arithmetic and copies ran while one was open for 11% of the time, Pallas kernels for 0%

profile of v1, /device:TPU:0, one launch (start us, length us, event | category | flops | bytes accessed | tf_op | source)
XLA Modules:
  0.0 264.3 jit_solution(2077956671415172602)
XLA Ops:
  0.0 1.2 copy.33
  1.3 3.1 %collective-permute-start = (f32[256,128]{0,1:T(8,128)S(1)}, f32[256,128]{0,1:T(8,128)S(1)}, u32[]{:S(2)}, u32[]{:S(2)}) collective-permute-start(f32[256,128]{0,1:T(8,128)S(1)} %get-tuple-element.14), channel_id=1, source_target_pairs={{0,4},{4,8},{8,12},{12,16},{16,20},{20,24},{24,28},{28,0},{1,5},{5... | collective-permute-start | bytes 393224 | tf_op jit(solution)/shard_map/ppermute | solution.py:16
  4.4 3.1 %collective-permute-start.1 = (f32[256,128]{0,1:T(8,128)S(1)}, f32[256,128]{0,1:T(8,128)S(1)}, u32[]{:S(2)}, u32[]{:S(2)}) collective-permute-start(f32[256,128]{0,1:T(8,128)S(1)} %get-tuple-element.15), channel_id=1, source_target_pairs={{0,28},{4,0},{8,4},{12,8},{16,12},{20,16},{24,20},{28,24},{1,29},{... | collective-permute-start | bytes 393224 | tf_op jit(solution)/shard_map/ppermute | solution.py:16
  7.5 0.7 collective-permute-start.3
  8.1 0.8 slice_bitcast_fusion.3
  9.0 0.5 compare_and_fusion.3
  9.5 0.5 compare_and_fusion.2
  10.1 0.5 compare_and_fusion
  10.6 0.5 compare_and_fusion.1
  11.2 0.5 and_bitcast_fusion
  11.7 0.6 compare_and_fusion.4
  12.4 37.7 %all-reduce = s32[256]{0:T(256)S(1)} all-reduce(s32[256]{0:T(256)S(1)} %bitcast_dynamic-update-slice_fusion), channel_id=2, replica_groups=mesh['sub'=8,'col'=4] {'sub','col'}, use_global_device_ids=true, to_apply=%add | all-reduce | flops 256 | bytes 2048
  50.1 0.5 compare_select_fusion.4
  50.7 0.6 pad_clamp_fusion
  51.3 0.7 gather_fusion.3
  52.1 0.6 fusion.39
  52.8 1.3 broadcast_select_fusion.9
  54.2 0.7 gather_fusion.1
  55.1 0.7 gather_fusion.2
  56.1 0.7 gather_fusion.4
  57.3 41.2 %all_gather.18 = bf16[256,128]{1,0:T(8,128)(2,1)S(1)} all-gather(bf16[8,128]{1,0:T(8,128)(2,1)S(1)} %fusion.9), channel_id=1, replica_groups=mesh['sub'=8,'col'=4] {'sub','col'}, dimensions={0}, use_global_device_ids=true | all-gather | bytes 67584 | tf_op jit(solution)/shard_map/all_gather | solution.py:60
  98.5 1.3 scatter_custom_fusion
  99.9 10.3 %psum.7 = bf16[32,128]{1,0:T(8,128)(2,1)S(1)} all-reduce(f32[32,128]{1,0:T(8,128)S(1)} %convolution_bitcast_fusion), channel_id=1, replica_groups=mesh['sub'=8,'col'=4] {'col'}, use_global_device_ids=true, to_apply=%region_1.3 | all-reduce | flops 4096 | bytes 24576 | tf_op jit(solution)/shard_map/psum | solution.py:67
  110.3 30.5 %all_gather.19 = bf16[256,128]{1,0:T(8,128)(2,1)S(1)} all-gather(bf16[32,128]{1,0:T(8,128)(2,1)S(1)} %psum.7), channel_id=1, replica_groups=mesh['sub'=8,'col'=4] {'sub'}, dimensions={0}, use_global_device_ids=true | all-gather | bytes 73728 | tf_op jit(solution)/shard_map/all_gather | solution.py:68
  140.8 1.6 fusion.2
  142.4 0.7 gather_fusion
  143.1 1.4 fusion.8
  144.5 0.7 fusion.34
  145.3 0.7 broadcast_select_fusion.10
  146.0 0.7 broadcast_select_fusion.11
  146.6 4.7 %collective-permute-start.5 = (f32[256,128]{0,1:T(8,128)}, f32[256,128]{0,1:T(8,128)S(1)}, u32[]{:S(2)}, u32[]{:S(2)}) collective-permute-start(f32[256,128]{0,1:T(8,128)} %get-tuple-element.13), channel_id=1, source_target_pairs={{0,28},{4,0},{8,4},{12,8},{16,12},{20,16},{24,20},{28,24},{1,29},{... | collective-permute-start | bytes 393224 | tf_op jit(solution)/shard_map/ppermute | solution.py:16
  151.3 0.5 collective-permute-start.6
  151.8 1.3 broadcast_select_fusion.8
  153.2 2.2 collective-permute-done.6
  155.4 0.7 gather_fusion.7
  156.4 0.7 gather_fusion.5
  157.3 0.7 gather_fusion.6
  158.2 1.0 copy.47
  159.2 0.7 gather_fusion.8
  160.0 0.8 broadcast_select_fusion.6
  160.8 0.7 broadcast_select_fusion.4
  161.6 0.8 fusion.4
  162.5 0.7 fusion.33
  163.3 2.0 collective-permute-start.9
  165.3 1.4 collective-permute-start.11
  166.7 0.9 copy.53
  167.7 1.3 gather_fusion.11
  169.0 1.0 copy.54
  170.0 1.3 broadcast_select_fusion.1
  171.3 1.0 copy.51
  172.3 1.3 gather_fusion.10
  173.7 1.0 copy.52
  174.7 1.3 broadcast_select_fusion.2
  175.9 1.0 copy.49
  176.9 1.3 gather_fusion.9
  178.3 1.0 copy.50
  179.3 0.7 broadcast_select_fusion.3
  179.9 1.0 copy.55
  180.9 1.3 gather_fusion.12
  182.3 1.0 copy.56
  183.3 1.5 fusion.15
  184.8 41.8 %all-gather.3 = f32[32,1,128]{2,1,0:T(1,128)S(1)} all-gather(f32[1,1,128]{2,1,0:T(1,128)S(1)} %multiply_bitcast_fusion.1), channel_id=3, replica_groups=mesh['sub'=8,'col'=4] {'sub','col'}, dimensions={0}, use_global_device_ids=true | all-gather | bytes 16896 | tf_op jit(solution)/shard_map/all_gather | solution.py:8
  226.6 36.7 %all-gather.4 = f32[32,1,128]{2,1,0:T(1,128)S(1)} all-gather(f32[1,1,128]{2,1,0:T(1,128)S(1)} %multiply_bitcast_fusion), channel_id=4, replica_groups=mesh['sub'=8,'col'=4] {'sub','col'}, dimensions={0}, use_global_device_ids=true | all-gather | bytes 16896 | tf_op jit(solution)/shard_map/all_gather | solution.py:8
  263.5 0.8 copy.57
  (87 shorter events, 2.5 us)
Async XLA Ops:
  0.0 140.8 %copy-start = (bf16[1,1024,1024]{2,1,0:T(8,128)(2,1)S(1)}, bf16[1,1024,1024]{2,1,0:T(8,128)(2,1)}, u32[]{:S(2)}) copy-start(bf16[1,1024,1024]{2,1,0:T(8,128)(2,1)} %param.11) | copy-start | bytes 6291460
  0.0 9.0 %copy-start.9 = (s32[1,1024]{1,0:T(1,128)S(1)}, s32[1,1024]{1,0:T(1,128)}, u32[]{:S(2)}) copy-start(s32[1,1024]{1,0:T(1,128)} %param.15) | copy-start | bytes 12292
  0.0 11.1 %copy-start.12 = (s32[1,8]{1,0:T(1,128)S(1)}, s32[1,8]{1,0:T(1,128)}, u32[]{:S(2)}) copy-start(s32[1,8]{1,0:T(1,128)} %param.14) | copy-start | bytes 100
  1.3 52.7 %collective-permute-start = (f32[256,128]{0,1:T(8,128)S(1)}, f32[256,128]{0,1:T(8,128)S(1)}, u32[]{:S(2)}, u32[]{:S(2)}) collective-permute-start(f32[256,128]{0,1:T(8,128)S(1)} %get-tuple-element.14), channel_id=1, source_target_pairs={{0,4},{4,8},{8,12},{12,16},{16,20},{20,24},{24,28},{28,0},{1,5},{5... | collective-permute-start | bytes 393224 | tf_op jit(solution)/shard_map/ppermute | solution.py:16
  4.4 50.6 %collective-permute-start.1 = (f32[256,128]{0,1:T(8,128)S(1)}, f32[256,128]{0,1:T(8,128)S(1)}, u32[]{:S(2)}, u32[]{:S(2)}) collective-permute-start(f32[256,128]{0,1:T(8,128)S(1)} %get-tuple-element.15), channel_id=1, source_target_pairs={{0,28},{4,0},{8,4},{12,8},{16,12},{20,16},{24,20},{28,24},{1,29},{... | collective-permute-start | bytes 393224 | tf_op jit(solution)/shard_map/ppermute | solution.py:16
  7.5 48.5 %collective-permute-start.3 = (f32[256,128]{0,1:T(8,128)S(1)}, f32[256,128]{0,1:T(8,128)S(1)}, u32[]{:S(2)}, u32[]{:S(2)}) collective-permute-start(f32[256,128]{0,1:T(8,128)S(1)} %get-tuple-element.16), channel_id=1, source_target_pairs={{0,3},{1,0},{2,1},{3,2},{4,7},{5,4},{6,5},{7,6},{8,11},{9,8},{10,9... | collective-permute-start | bytes 393224 | tf_op jit(solution)/shard_map/ppermute | solution.py:16
  9.0 42.3 %collective-permute-start.2 = (bf16[256,128]{1,0:T(8,128)(2,1)S(1)}, bf16[256,128]{1,0:T(8,128)(2,1)S(1)}, u32[]{:S(2)}, u32[]{:S(2)}) collective-permute-start(bf16[256,128]{1,0:T(8,128)(2,1)S(1)} %slice_bitcast_fusion.3), channel_id=1, source_target_pairs={{0,1},{1,2},{2,3},{3,0},{4,5},{5,6},{6,7},{7,4},{8,9},{9,10},{10,1... | collective-permute-start | bytes 196616 | tf_op jit(solution)/shard_map/ppermute | solution.py:16
  54.9 2.0 copy-start.6
  54.9 2.1 copy-start.8
  54.9 2.1 copy-start.4
  55.9 1.3 copy-start.2
  55.9 43.9 %copy-start.3 = (bf16[32,64]{1,0:T(8,128)(2,1)S(1)}, bf16[32,64]{1,0:T(8,128)(2,1)}, u32[]{:S(2)}) copy-start(bf16[32,64]{1,0:T(8,128)(2,1)} %param.13) | copy-start | bytes 12292
  57.0 86.1 %copy-start.10 = (pred[8]{0:T(512)(128)(4,1)S(1)}, pred[8]{0:T(512)(128)(4,1)}, u32[]{:S(2)}) copy-start(pred[8]{0:T(512)(128)(4,1)} %and_bitcast_fusion) | copy-start | bytes 28
  57.0 86.1 %copy-start.11 = (pred[8]{0:T(512)(128)(4,1)S(1)}, pred[8]{0:T(512)(128)(4,1)}, u32[]{:S(2)}) copy-start(pred[8]{0:T(512)(128)(4,1)} %compare_and_fusion.4) | copy-start | bytes 28
  146.6 9.7 %collective-permute-start.4 = (f32[256,128]{0,1:T(8,128)}, f32[256,128]{0,1:T(8,128)S(1)}, u32[]{:S(2)}, u32[]{:S(2)}) collective-permute-start(f32[256,128]{0,1:T(8,128)} %get-tuple-element.11), channel_id=1, source_target_pairs={{0,4},{4,8},{8,12},{12,16},{16,20},{20,24},{24,28},{28,0},{1,5},{5... | collective-permute-start | bytes 393224 | tf_op jit(solution)/shard_map/ppermute | solution.py:16
  146.6 10.6 %collective-permute-start.5 = (f32[256,128]{0,1:T(8,128)}, f32[256,128]{0,1:T(8,128)S(1)}, u32[]{:S(2)}, u32[]{:S(2)}) collective-permute-start(f32[256,128]{0,1:T(8,128)} %get-tuple-element.13), channel_id=1, source_target_pairs={{0,28},{4,0},{8,4},{12,8},{16,12},{20,16},{24,20},{28,24},{1,29},{... | collective-permute-start | bytes 393224 | tf_op jit(solution)/shard_map/ppermute | solution.py:16
  151.3 6.8 %collective-permute-start.7 = (f32[256,128]{0,1:T(8,128)}, f32[256,128]{0,1:T(8,128)}, u32[]{:S(2)}, u32[]{:S(2)}) collective-permute-start(f32[256,128]{0,1:T(8,128)} %get-tuple-element.12), channel_id=1, source_target_pairs={{0,3},{1,0},{2,1},{3,2},{4,7},{5,4},{6,5},{7,6},{8,11},{9,8},{10,9... | collective-permute-start | bytes 393224 | tf_op jit(solution)/shard_map/ppermute | solution.py:16
  151.3 4.0 %collective-permute-start.6 = (bf16[256,128]{0,1:T(8,128)(2,1)S(1)}, bf16[256,128]{0,1:T(8,128)(2,1)S(1)}, u32[]{:S(2)}, u32[]{:S(2)}) collective-permute-start(bf16[256,128]{0,1:T(8,128)(2,1)S(1)} %slice.134), channel_id=1, source_target_pairs={{0,1},{1,2},{2,3},{3,0},{4,5},{5,6},{6,7},{7,4},{8,9},{9,10},{10,1... | collective-permute-start | bytes 196616 | tf_op jit(solution)/shard_map/ppermute | solution.py:16
  160.0 1.6 copy-start.1
  162.5 4.2 %collective-permute-start.10 = (bf16[256,128]{0,1:T(8,128)(2,1)S(1)}, bf16[256,128]{0,1:T(8,128)(2,1)}, u32[]{:S(2)}, u32[]{:S(2)}) collective-permute-start(bf16[256,128]{0,1:T(8,128)(2,1)S(1)} %slice.133), channel_id=1, source_target_pairs={{0,1},{1,2},{2,3},{3,0},{4,5},{5,6},{6,7},{7,4},{8,9},{9,10},{10,1... | collective-permute-start | bytes 196616 | tf_op jit(solution)/shard_map/ppermute | solution.py:16
  163.3 8.0 %collective-permute-start.9 = (f32[256,128]{0,1:T(8,128)}, f32[256,128]{0,1:T(8,128)}, u32[]{:S(2)}, u32[]{:S(2)}) collective-permute-start(f32[256,128]{0,1:T(8,128)} %get-tuple-element.10), channel_id=1, source_target_pairs={{0,28},{4,0},{8,4},{12,8},{16,12},{20,16},{24,20},{28,24},{1,29},{... | collective-permute-start | bytes 393224 | tf_op jit(solution)/shard_map/ppermute | solution.py:16
  165.3 10.7 %collective-permute-start.8 = (f32[256,128]{0,1:T(8,128)}, f32[256,128]{0,1:T(8,128)}, u32[]{:S(2)}, u32[]{:S(2)}) collective-permute-start(f32[256,128]{0,1:T(8,128)} %get-tuple-element.8), channel_id=1, source_target_pairs={{0,4},{4,8},{8,12},{12,16},{16,20},{20,24},{24,28},{28,0},{1,5},{5... | collective-permute-start | bytes 393224 | tf_op jit(solution)/shard_map/ppermute | solution.py:16
  165.3 14.6 %collective-permute-start.11 = (f32[256,128]{0,1:T(8,128)}, f32[256,128]{0,1:T(8,128)}, u32[]{:S(2)}, u32[]{:S(2)}) collective-permute-start(f32[256,128]{0,1:T(8,128)} %get-tuple-element.9), channel_id=1, source_target_pairs={{0,3},{1,0},{2,1},{3,2},{4,7},{5,4},{6,5},{7,6},{8,11},{9,8},{10,9... | collective-permute-start | bytes 393224 | tf_op jit(solution)/shard_map/ppermute | solution.py:16
  169.0 10.3 %copy-start.7 = (pred[256]{0:T(512)(128)(4,1)S(1)}, pred[256]{0:T(512)(128)(4,1)}, u32[]{:S(2)}) copy-start(pred[256]{0:T(512)(128)(4,1)} %compare_and_fusion.3) | copy-start | bytes 772
  173.6 9.6 %copy-start.5 = (pred[256]{0:T(512)(128)(4,1)S(1)}, pred[256]{0:T(512)(128)(4,1)}, u32[]{:S(2)}) copy-start(pred[256]{0:T(512)(128)(4,1)} %compare_and_fusion) | copy-start | bytes 772
